TPU v7x, 32 devices: a whole 2x2x4 slice. The times are simulated.
32 devices in a mesh: dp: 16 (over z, x, core), tensor: 2 (over y).
Axes of the slice: x: 2, y: 2, z: 4, core: 2. Of those that a mesh axis runs over, the one named last changes fastest.
Arguments:
- entering_activations: float32 [16384, 1024], P(('dp', 'tensor')), may hold values from -6 to 6
- segment_ids: int32 [16, 1024], P('dp'), may hold values from 0 to 7, never falling along the last dimension, each value on 1 to 512 neighbouring positions
- leaving_activation_slope: float32 [16384, 1024], P(('dp', 'tensor')), may hold values from -6 to 6
- qkv_weight: float32 [1024, 3072], P('dp', 'tensor'), may hold values from -0.1875 to 0.1875
- qv_bias: float32 [2048], P('tensor'), may hold values from -1.75 to 1.75
- dense_weight: float32 [1024, 1024], P('tensor', 'dp'), may hold values from -0.5 to 0.5
- dense_bias: float32 [1024], replicated, may hold values from -1.75 to 1.75
- up_weight: float32 [1024, 4096], P('dp', 'tensor'), may hold values from -0.1875 to 0.1875
- up_bias: float32 [4096], P('tensor'), may hold values from -3 to 3
- down_weight: float32 [4096, 1024], P('tensor', 'dp'), may hold values from -0.09375 to 0.09375
- down_bias: float32 [1024], replicated, may hold values from -1.75 to 1.75
- mixer_scale_factor: float32 [1024], replicated, may hold values from 0.1 to 1.9
- mixer_offset_term: float32 [1024], replicated, may hold values from -1.75 to 1.75
- perceptron_scale_factor: float32 [1024], replicated, may hold values from 0.1 to 1.9
- perceptron_offset_term: float32 [1024], replicated, may hold values from -1.75 to 1.75
- first_qkv_weight: float32 [1024, 3072], P('dp', 'tensor'), may hold values from -24 to 24
- first_qv_bias: float32 [2048], P('tensor'), may hold values from -24 to 24
- first_dense_weight: float32 [1024, 1024], P('tensor', 'dp'), may hold values from -24 to 24
- first_dense_bias: float32 [1024], replicated, may hold values from -64 to 64
- first_up_weight: float32 [1024, 4096], P('dp', 'tensor'), may hold values from -24 to 24
- first_up_bias: float32 [4096], P('tensor'), may hold values from -24 to 24
- first_down_weight: float32 [4096, 1024], P('tensor', 'dp'), may hold values from -24 to 24
- first_down_bias: float32 [1024], replicated, may hold values from -64 to 64
- first_norm1_gain: float32 [1024], replicated, may hold values from -64 to 64
- first_norm1_bias: float32 [1024], replicated, may hold values from -64 to 64
- first_norm2_gain: float32 [1024], replicated, may hold values from -64 to 64
- first_norm2_bias: float32 [1024], replicated, may hold values from -64 to 64
- second_qkv_weight: float32 [1024, 3072], P('dp', 'tensor'), may hold values from 64 to 2048
- second_qv_bias: float32 [2048], P('tensor'), may hold values from 64 to 2048
- second_dense_weight: float32 [1024, 1024], P('tensor', 'dp'), may hold values from 64 to 2048
- second_dense_bias: float32 [1024], replicated, may hold values from 1024 to 16384
- second_up_weight: float32 [1024, 4096], P('dp', 'tensor'), may hold values from 64 to 2048
- second_up_bias: float32 [4096], P('tensor'), may hold values from 64 to 2048
- second_down_weight: float32 [4096, 1024], P('tensor', 'dp'), may hold values from 64 to 2048
- second_down_bias: float32 [1024], replicated, may hold values from 1024 to 16384
- second_norm1_gain: float32 [1024], replicated, may hold values from 1024 to 16384
- second_norm1_bias: float32 [1024], replicated, may hold values from 1024 to 16384
- second_norm2_gain: float32 [1024], replicated, may hold values from 1024 to 16384
- second_norm2_bias: float32 [1024], replicated, may hold values from 1024 to 16384
Outputs:
- block_out: float32 [16384, 1024], P(('dp', 'tensor'))
- entering_activation_slope: float32 [16384, 1024], P(('dp', 'tensor'))
- grad_qkv_weight: float32 [1024, 3072], P('dp', 'tensor')
- grad_qv_bias: float32 [2048], P('tensor')
- grad_dense_weight: float32 [1024, 1024], P('tensor', 'dp')
- grad_dense_bias: float32 [1024], replicated
- grad_up_weight: float32 [1024, 4096], P('dp', 'tensor')
- grad_up_bias: float32 [4096], P('tensor')
- grad_down_weight: float32 [4096, 1024], P('tensor', 'dp')
- grad_down_bias: float32 [1024], replicated
- grad_norm1_gain: float32 [1024], replicated
- grad_norm1_bias: float32 [1024], replicated
- grad_norm2_gain: float32 [1024], replicated
- grad_norm2_bias: float32 [1024], replicated
- new_qkv_weight: float32 [1024, 3072], P('dp', 'tensor')
- new_qv_bias: float32 [2048], P('tensor')
- new_dense_weight: float32 [1024, 1024], P('tensor', 'dp')
- new_dense_bias: float32 [1024], replicated
- new_up_weight: float32 [1024, 4096], P('dp', 'tensor')
- new_up_bias: float32 [4096], P('tensor')
- new_down_weight: float32 [4096, 1024], P('tensor', 'dp')
- new_down_bias: float32 [1024], replicated
- new_norm1_gain: float32 [1024], replicated
- new_norm1_bias: float32 [1024], replicated
- new_norm2_gain: float32 [1024], replicated
- new_norm2_bias: float32 [1024], replicated
- new_first_qkv_weight: float32 [1024, 3072], P('dp', 'tensor')
- new_first_qv_bias: float32 [2048], P('tensor')
- new_first_dense_weight: float32 [1024, 1024], P('tensor', 'dp')
- new_first_dense_bias: float32 [1024], replicated
- new_first_up_weight: float32 [1024, 4096], P('dp', 'tensor')
- new_first_up_bias: float32 [4096], P('tensor')
- new_first_down_weight: float32 [4096, 1024], P('tensor', 'dp')
- new_first_down_bias: float32 [1024], replicated
- new_first_norm1_gain: float32 [1024], replicated
- new_first_norm1_bias: float32 [1024], replicated
- new_first_norm2_gain: float32 [1024], replicated
- new_first_norm2_bias: float32 [1024], replicated
- new_second_qkv_weight: float32 [1024, 3072], P('dp', 'tensor')
- new_second_qv_bias: float32 [2048], P('tensor')
- new_second_dense_weight: float32 [1024, 1024], P('tensor', 'dp')
- new_second_dense_bias: float32 [1024], replicated
- new_second_up_weight: float32 [1024, 4096], P('dp', 'tensor')
- new_second_up_bias: float32 [4096], P('tensor')
- new_second_down_weight: float32 [4096, 1024], P('tensor', 'dp')
- new_second_down_bias: float32 [1024], replicated
- new_second_norm1_gain: float32 [1024], replicated
- new_second_norm1_bias: float32 [1024], replicated
- new_second_norm2_gain: float32 [1024], replicated
- new_second_norm2_bias: float32 [1024], replicated
Inputs may be any that keep to these rules, and one draw needn't show every extreme that they name: Along each row of segment_ids the numbers never fall.
All inputs are finite; a program needn't handle non-finite values.
Results may differ from a plain program's by a relative error of at most 0.019.
Values may be sent and summed in bfloat16 or wider, within the bound.
A program may use at most 256 MiB of HBM per device.

v0:
```python
import jax
import jax.numpy as jnp
from jax import lax
from jax.sharding import PartitionSpec as P

D = 1024
FOCUS_COUNT = 16
FF = 4096
ADAM_STEP = 4
HEAD_DIM = 64


beta_first = 0.9
beta_second = 0.95


def standardise_features(values, elementwise_multiplier, additive_offset):
    feature_midpoint = jnp.mean(values, axis=-1, keepdims=True)
    demeaned_entries = values - feature_midpoint
    reciprocal_spread = lax.rsqrt(
        jnp.mean(demeaned_entries * demeaned_entries, axis=-1, keepdims=True) + 1e-05
    )
    unit_spread_entries = demeaned_entries * reciprocal_spread
    return (
        (unit_spread_entries * elementwise_multiplier + additive_offset).astype(jnp.bfloat16),
        unit_spread_entries,
        reciprocal_spread,
    )


def standardise_features_reverse(
    loss_slope, unit_spread_entries, reciprocal_spread, elementwise_multiplier
):
    multiplied_entries = loss_slope * elementwise_multiplier
    return reciprocal_spread * (
        multiplied_entries
        - jnp.mean(multiplied_entries, axis=-1, keepdims=True)
        - unit_spread_entries
        * jnp.mean(multiplied_entries * unit_spread_entries, axis=-1, keepdims=True)
    )


def gelu_parts(pre):
    inner = 0.7978845608 * (pre + 0.044715 * pre * pre * pre)
    tanh_val = jnp.tanh(inner)
    value = 0.5 * pre * (1.0 + tanh_val)
    slope = 0.5 * (1.0 + tanh_val) + 0.5 * pre * (1.0 - tanh_val * tanh_val) * 0.7978845608 * (
        1.0 + 3.0 * 0.044715 * pre * pre
    )
    return (value, slope)


def inner_rows(left, right):
    return lax.dot_general(
        left, right, (((0,), (0,)), ((), ())), preferred_element_type=jnp.float32
    )


def times_transposed(left, right):
    return lax.dot_general(
        left, right, (((1,), (1,)), ((), ())), preferred_element_type=jnp.float32
    )


def head_slopes(first, count):
    index = (first + jnp.arange(count)).astype(jnp.float32)
    return jnp.exp2(-8.0 * (index + 1.0) / FOCUS_COUNT)


def full_bias(qv_bias, heads):
    pair = qv_bias.reshape(heads, 2, HEAD_DIM)
    return jnp.stack([pair[:, 0], jnp.zeros_like(pair[:, 0]), pair[:, 1]], axis=1).reshape(
        heads * 3 * HEAD_DIM
    )


def masked_scores(query, keys, start, segments, slopes):
    block = query.shape[0]
    length = keys.shape[0]
    raw = jnp.einsum(
        "qhd,khd->hqk", query, keys, preferred_element_type=jnp.float32
    ) * HEAD_DIM ** (-0.5)
    rows = start + jnp.arange(block)
    cols = jnp.arange(length)
    offset = (cols[None, :] - rows[:, None]).astype(jnp.float32)
    seg_rows = segments[start : start + block]
    allowed = (cols[None, :] <= rows[:, None]) & (seg_rows[:, None] == segments[None, :])
    return jnp.where(allowed[None], raw + slopes[:, None, None] * offset[None], -1e30)


def split_heads(qkv_low):
    length = qkv_low.shape[0]
    heads = qkv_low.shape[1] // (3 * HEAD_DIM)
    split = qkv_low.reshape(length, heads, 3, HEAD_DIM)
    return (split[:, :, 0], split[:, :, 1], split[:, :, 2], heads)


def attention_forward(qkv_low, segments, slopes):
    query, keys, values, heads = split_heads(qkv_low)
    length = query.shape[0]
    block = min(512, length)
    contexts = []
    totals = []
    for start in range(0, length, block):
        scores = masked_scores(query[start : start + block], keys, start, segments, slopes)
        peak = jnp.max(scores, axis=-1, keepdims=True)
        total = peak + jnp.log(jnp.sum(jnp.exp(scores - peak), axis=-1, keepdims=True))
        probs = jnp.exp(scores - total).astype(jnp.bfloat16)
        context = jnp.einsum("hqk,khd->qhd", probs, values, preferred_element_type=jnp.float32)
        contexts.append(context.reshape(block, heads * HEAD_DIM).astype(jnp.bfloat16))
        totals.append(total)
    return (jnp.concatenate(contexts, axis=0), totals)


def attention_backward(qkv_low, segments, slopes, totals, dcontext):
    query, keys, values, heads = split_heads(qkv_low)
    length = query.shape[0]
    block = min(512, length)
    scale = HEAD_DIM ** (-0.5)
    dkeys = jnp.zeros(keys.shape, jnp.float32)
    dvalues = jnp.zeros(values.shape, jnp.float32)
    dquery_parts = []
    for number, start in enumerate(range(0, length, block)):
        query_block = query[start : start + block]
        scores = masked_scores(query_block, keys, start, segments, slopes)
        probs = jnp.exp(scores - totals[number])
        probs_low = probs.astype(jnp.bfloat16)
        grad_block = dcontext[start : start + block].reshape(block, heads, HEAD_DIM)
        dvalues = dvalues + jnp.einsum(
            "hqk,qhd->khd", probs_low, grad_block, preferred_element_type=jnp.float32
        )
        dprob = jnp.einsum("qhd,khd->hqk", grad_block, values, preferred_element_type=jnp.float32)
        delta = jnp.sum(probs * dprob, axis=-1, keepdims=True)
        dscore = (probs * (dprob - delta)).astype(jnp.bfloat16)
        dquery_parts.append(
            jnp.einsum("hqk,khd->qhd", dscore, keys, preferred_element_type=jnp.float32) * scale
        )
        dkeys = (
            dkeys
            + jnp.einsum("hqk,qhd->khd", dscore, query_block, preferred_element_type=jnp.float32)
            * scale
        )
    dquery = jnp.concatenate(dquery_parts, axis=0)
    return jnp.stack([dquery, dkeys, dvalues], axis=2).reshape(length, heads * 3 * HEAD_DIM)


def query_value_slope(packed_triple_sensitivity, heads):
    split = packed_triple_sensitivity.reshape(
        packed_triple_sensitivity.shape[0], heads, 3, HEAD_DIM
    )
    pair = jnp.stack([split[:, :, 0], split[:, :, 2]], axis=2)
    return jnp.sum(pair, axis=0).reshape(heads * 2 * HEAD_DIM)


def adamw(param, loss_slope, first, second, rate, decay):
    first_new = beta_first * first + (1.0 - beta_first) * loss_slope
    second_new = beta_second * second + (1.0 - beta_second) * loss_slope * loss_slope
    update = (
        first_new
        / (1.0 - beta_first**ADAM_STEP)
        / (jnp.sqrt(second_new / (1.0 - beta_second**ADAM_STEP)) + 1e-08)
    )
    return (param - rate * (update + decay * param), first_new, second_new)


def local(
    entering_activations,
    segment_ids,
    leaving_activation_slope,
    qkv_weight,
    qv_bias,
    dense_weight,
    dense_bias,
    up_weight,
    up_bias,
    down_weight,
    down_bias,
    mixer_scale_factor,
    mixer_offset_term,
    perceptron_scale_factor,
    perceptron_offset_term,
    first_qkv_weight,
    first_qv_bias,
    first_dense_weight,
    first_dense_bias,
    first_up_weight,
    first_up_bias,
    first_down_weight,
    first_down_bias,
    first_norm1_gain,
    first_norm1_bias,
    first_norm2_gain,
    first_norm2_bias,
    second_qkv_weight,
    second_qv_bias,
    second_dense_weight,
    second_dense_bias,
    second_up_weight,
    second_up_bias,
    second_down_weight,
    second_down_bias,
    second_norm1_gain,
    second_norm1_bias,
    second_norm2_gain,
    second_norm2_bias,
):
    params = (
        qkv_weight,
        qv_bias,
        dense_weight,
        dense_bias,
        up_weight,
        up_bias,
        down_weight,
        down_bias,
        mixer_scale_factor,
        mixer_offset_term,
        perceptron_scale_factor,
        perceptron_offset_term,
    )
    firsts = (
        first_qkv_weight,
        first_qv_bias,
        first_dense_weight,
        first_dense_bias,
        first_up_weight,
        first_up_bias,
        first_down_weight,
        first_down_bias,
        first_norm1_gain,
        first_norm1_bias,
        first_norm2_gain,
        first_norm2_bias,
    )
    seconds = (
        second_qkv_weight,
        second_qv_bias,
        second_dense_weight,
        second_dense_bias,
        second_up_weight,
        second_up_bias,
        second_down_weight,
        second_down_bias,
        second_norm1_gain,
        second_norm1_bias,
        second_norm2_gain,
        second_norm2_bias,
    )
    qkv_low, dense_low, up_low, down_low = (
        lax.all_gather(qkv_weight.astype(jnp.bfloat16), "dp", axis=0, tiled=True),
        lax.all_gather(dense_weight.astype(jnp.bfloat16), "dp", axis=1, tiled=True),
        lax.all_gather(up_weight.astype(jnp.bfloat16), "dp", axis=0, tiled=True),
        lax.all_gather(down_weight.astype(jnp.bfloat16), "dp", axis=1, tiled=True),
    )
    local_heads = qkv_low.shape[1] // (3 * HEAD_DIM)
    tensor_rank = lax.axis_index("tensor")
    slopes = head_slopes(tensor_rank * local_heads, local_heads)
    segments = segment_ids[0]
    mixer_standardised, mixer_unit_spread1, mixer_reciprocal_spread1 = standardise_features(
        entering_activations, mixer_scale_factor, mixer_offset_term
    )
    full_one = lax.all_gather(mixer_standardised, "tensor", axis=0, tiled=True)
    qkv = (
        jnp.dot(full_one, qkv_low, preferred_element_type=jnp.float32)
        + full_bias(qv_bias, local_heads)
    ).astype(jnp.bfloat16)
    context, totals = attention_forward(qkv, segments, slopes)
    skip_path_sum = (
        entering_activations
        + lax.psum_scatter(
            jnp.dot(context, dense_low, preferred_element_type=jnp.float32).astype(jnp.bfloat16),
            "tensor",
            scatter_dimension=0,
            tiled=True,
        ).astype(jnp.float32)
        + dense_bias
    )
    perceptron_standardised, perceptron_unit_spread2, perceptron_reciprocal_spread2 = (
        standardise_features(skip_path_sum, perceptron_scale_factor, perceptron_offset_term)
    )
    full_two = lax.all_gather(perceptron_standardised, "tensor", axis=0, tiled=True)
    pre = jnp.dot(full_two, up_low, preferred_element_type=jnp.float32) + up_bias
    act_val, act_slope = gelu_parts(pre)
    act = act_val.astype(jnp.bfloat16)
    block_out = (
        skip_path_sum
        + lax.psum_scatter(
            jnp.dot(act, down_low, preferred_element_type=jnp.float32).astype(jnp.bfloat16),
            "tensor",
            scatter_dimension=0,
            tiled=True,
        ).astype(jnp.float32)
        + down_bias
    )
    full_out = lax.all_gather(
        leaving_activation_slope.astype(jnp.bfloat16), "tensor", axis=0, tiled=True
    )
    contraction_sensitivity = inner_rows(act, full_out)
    hidden_activation_sensitivity = times_transposed(full_out, down_low) * act_slope
    dpre_low = hidden_activation_sensitivity.astype(jnp.bfloat16)
    expansion_sensitivity = inner_rows(full_two, dpre_low)
    up_bias_part = jnp.sum(hidden_activation_sensitivity, axis=0)
    pre_perceptron_sensitivity = lax.psum_scatter(
        times_transposed(dpre_low, up_low).astype(jnp.bfloat16),
        "tensor",
        scatter_dimension=0,
        tiled=True,
    ).astype(jnp.float32)
    skip_path_sensitivity = leaving_activation_slope + standardise_features_reverse(
        pre_perceptron_sensitivity,
        perceptron_unit_spread2,
        perceptron_reciprocal_spread2,
        perceptron_scale_factor,
    )
    full_resid = lax.all_gather(
        skip_path_sensitivity.astype(jnp.bfloat16), "tensor", axis=0, tiled=True
    )
    mixer_merge_sensitivity = inner_rows(context, full_resid)
    dcontext = times_transposed(full_resid, dense_low).astype(jnp.bfloat16)
    packed_triple_sensitivity = attention_backward(qkv, segments, slopes, totals, dcontext)
    dqkv_low = packed_triple_sensitivity.astype(jnp.bfloat16)
    packed_triple_slope = inner_rows(full_one, dqkv_low)
    qv_part = query_value_slope(packed_triple_sensitivity, local_heads)
    pre_mixer_sensitivity = lax.psum_scatter(
        times_transposed(dqkv_low, qkv_low).astype(jnp.bfloat16),
        "tensor",
        scatter_dimension=0,
        tiled=True,
    ).astype(jnp.float32)
    entering_activation_slope = skip_path_sensitivity + standardise_features_reverse(
        pre_mixer_sensitivity, mixer_unit_spread1, mixer_reciprocal_spread1, mixer_scale_factor
    )
    packed_triple_slope, mixer_merge_sensitivity, expansion_sensitivity, contraction_sensitivity = (
        lax.psum_scatter(packed_triple_slope, "dp", scatter_dimension=0, tiled=True),
        lax.psum_scatter(mixer_merge_sensitivity, "dp", scatter_dimension=1, tiled=True),
        lax.psum_scatter(expansion_sensitivity, "dp", scatter_dimension=0, tiled=True),
        lax.psum_scatter(contraction_sensitivity, "dp", scatter_dimension=1, tiled=True),
    )
    qv_width = qv_part.shape[0]
    up_width = up_bias_part.shape[0]
    qv_spread = lax.dynamic_update_slice_in_dim(
        jnp.zeros((2 * D,), jnp.float32), qv_part, tensor_rank * qv_width, 0
    )
    up_spread = lax.dynamic_update_slice_in_dim(
        jnp.zeros((FF,), jnp.float32), up_bias_part, tensor_rank * up_width, 0
    )
    sums = lax.psum(
        (
            jnp.sum(skip_path_sensitivity, axis=0),
            jnp.sum(leaving_activation_slope, axis=0),
            jnp.sum(pre_mixer_sensitivity * mixer_unit_spread1, axis=0),
            jnp.sum(pre_mixer_sensitivity, axis=0),
            jnp.sum(pre_perceptron_sensitivity * perceptron_unit_spread2, axis=0),
            jnp.sum(pre_perceptron_sensitivity, axis=0),
            qv_spread,
            up_spread,
        ),
        ("dp", "tensor"),
    )
    (
        dense_bias_grad,
        down_bias_grad,
        gain_one_grad,
        shift_one_grad,
        gain_two_grad,
        shift_two_grad,
        qv_total,
        up_total,
    ) = sums
    qv_bias_grad = lax.dynamic_slice_in_dim(qv_total, tensor_rank * qv_width, qv_width, 0)
    up_bias_grad = lax.dynamic_slice_in_dim(up_total, tensor_rank * up_width, up_width, 0)
    parameter_slopes = (
        packed_triple_slope,
        qv_bias_grad,
        mixer_merge_sensitivity,
        dense_bias_grad,
        expansion_sensitivity,
        up_bias_grad,
        contraction_sensitivity,
        down_bias_grad,
        gain_one_grad,
        shift_one_grad,
        gain_two_grad,
        shift_two_grad,
    )
    results = []
    for index in range(12):
        matrix = index in (0, 2, 4, 6)
        results.append(
            adamw(
                params[index],
                parameter_slopes[index],
                firsts[index],
                seconds[index],
                0.01 if matrix else 0.1,
                0.1 if matrix else 0.0,
            )
        )
    news = [r[0] for r in results]
    moments_one = [r[1] for r in results]
    moments_two = [r[2] for r in results]
    return (
        block_out,
        entering_activation_slope,
        *parameter_slopes,
        *news,
        *moments_one,
        *moments_two,
    )


def solution(mesh):
    in_specs = (
        P(("dp", "tensor"), None),
        P("dp", None),
        P(("dp", "tensor"), None),
        P("dp", "tensor"),
        P("tensor"),
        P("tensor", "dp"),
        P(),
        P("dp", "tensor"),
        P("tensor"),
        P("tensor", "dp"),
        P(),
        P(),
        P(),
        P(),
        P(),
        P("dp", "tensor"),
        P("tensor"),
        P("tensor", "dp"),
        P(),
        P("dp", "tensor"),
        P("tensor"),
        P("tensor", "dp"),
        P(),
        P(),
        P(),
        P(),
        P(),
        P("dp", "tensor"),
        P("tensor"),
        P("tensor", "dp"),
        P(),
        P("dp", "tensor"),
        P("tensor"),
        P("tensor", "dp"),
        P(),
        P(),
        P(),
        P(),
        P(),
    )
    out_specs = (
        P(("dp", "tensor"), None),
        P(("dp", "tensor"), None),
        P("dp", "tensor"),
        P("tensor"),
        P("tensor", "dp"),
        P(),
        P("dp", "tensor"),
        P("tensor"),
        P("tensor", "dp"),
        P(),
        P(),
        P(),
        P(),
        P(),
        P("dp", "tensor"),
        P("tensor"),
        P("tensor", "dp"),
        P(),
        P("dp", "tensor"),
        P("tensor"),
        P("tensor", "dp"),
        P(),
        P(),
        P(),
        P(),
        P(),
        P("dp", "tensor"),
        P("tensor"),
        P("tensor", "dp"),
        P(),
        P("dp", "tensor"),
        P("tensor"),
        P("tensor", "dp"),
        P(),
        P(),
        P(),
        P(),
        P(),
        P("dp", "tensor"),
        P("tensor"),
        P("tensor", "dp"),
        P(),
        P("dp", "tensor"),
        P("tensor"),
        P("tensor", "dp"),
        P(),
        P(),
        P(),
        P(),
        P(),
    )
    return jax.shard_map(local, mesh=mesh, in_specs=in_specs, out_specs=out_specs, check_vma=False)
```

profile of v0, /device:TPU:0, one launch (start us, length us, event | category | flops | bytes accessed | tf_op | source)
XLA Modules:
  0.0 939.6 jit_solution(16158971686798372823)
XLA Ops:
  18.2 29.8 %all-gather.9.cloned.1.call-done = bf16[1024,1024]{1,0:T(8,128)(2,1)} async-done(((bf16[512,1024]{1,0:T(8,128)(2,1)}), bf16[1024,1024]{1,0:T(8,128)(2,1)}) %all-gather.9.cloned.1.call-update) | async-done | bytes 2097168 | tf_op jit(solution)/shard_map/all_gather | solution.py:262
  48.0 48.4 %all-gather.11.cloned.1.call-done = bf16[1024,1536]{1,0:T(8,128)(2,1)} async-done(((bf16[64,1536]{1,0:T(8,128)(2,1)}), bf16[1024,1536]{1,0:T(8,128)(2,1)}) %all-gather.11.cloned.1.call-update) | async-done | bytes 3145744 | tf_op jit(solution)/shard_map/all_gather | solution.py:250
  140.6 8.2 fusion.46
  153.7 29.7 %reduce-scatter.9.cloned.1.call-done = bf16[512,1024]{1,0:T(8,128)(2,1)} async-done(((bf16[1024,1024]{1,0:T(8,128)(2,1)}), bf16[512,1024]{1,0:T(8,128)(2,1)}) %reduce-scatter.9.cloned.1.call-update) | async-done | bytes 1048592 | tf_op jit(solution)/shard_map/reduce_scatter | solution.py:270
  189.8 46.6 %all-gather.17.cloned.1.call-done = bf16[1024,2048]{1,0:T(8,128)(2,1)} async-done(((bf16[64,2048]{1,0:T(8,128)(2,1)}), bf16[1024,2048]{1,0:T(8,128)(2,1)}) %all-gather.17.cloned.1.call-update) | async-done | bytes 4194320 | tf_op jit(solution)/shard_map/all_gather | solution.py:252
  236.4 33.6 %all-gather.15.cloned.1.call-done = bf16[1024,1024]{1,0:T(8,128)(2,1)} async-done(((bf16[512,1024]{1,0:T(8,128)(2,1)}), bf16[1024,1024]{1,0:T(8,128)(2,1)}) %all-gather.15.cloned.1.call-update) | async-done | bytes 2097168 | tf_op jit(solution)/shard_map/all_gather | solution.py:281
  270.0 10.9 %fusion.95 = f32[1024,2048]{1,0:T(8,128)} fusion(bf16[1024,1024]{1,0:T(8,128)(2,1)} %all-gather.15.cloned.1.call-done, bf16[1024,2048]{1,0:T(8,128)(2,1)} %all-gather.17.cloned.1.call-done), kind=kOutput, calls=%fused_computation.167 | convolution fusion | flops 4294967296 | bytes 14680064 | tf_op jit(solution)/shard_map/dot_general | solution.py:282
  280.9 23.8 %all-gather.21.cloned.1.call-done = bf16[1024,1024]{1,0:T(8,128)(2,1)} async-done(((bf16[512,1024]{1,0:T(8,128)(2,1)}), bf16[1024,1024]{1,0:T(8,128)(2,1)}) %all-gather.21.cloned.1.call-update) | async-done | bytes 2097168 | tf_op jit(solution)/shard_map/all_gather | solution.py:295
  304.7 12.0 %fusion.71 = f32[2048,1024]{0,1:T(8,128)} fusion(bf16[1024,1024]{1,0:T(8,128)(2,1)} %all-gather.21.cloned.1.call-done, f32[1024,2048]{1,0:T(8,128)} %fusion.95, f32[2048]{0:T(1024)S(1)} %copy-done.64), kind=kOutput, calls=%fused_computation.156 | convolution fusion | flops 4315938816 | bytes 18882560 | tf_op jit(solution)/shard_map/dot_general | solution.py:54
  316.7 103.6 %reduce-scatter.23.cloned.1.call-done = f32[2048,64]{0,1:T(8,128)} async-done(((f32[2048,1024]{0,1:T(8,128)}), f32[2048,64]{0,1:T(8,128)}) %reduce-scatter.23.cloned.1.call-update) | async-done | bytes 524304 | tf_op jit(solution)/shard_map/reduce_scatter | solution.py:337
  423.3 49.8 %all-gather.19.cloned.1.call-done = bf16[2048,1024]{0,1:T(8,128)(2,1)} async-done(((bf16[2048,64]{0,1:T(8,128)(2,1)}), bf16[2048,1024]{0,1:T(8,128)(2,1)}) %all-gather.19.cloned.1.call-update) | async-done | bytes 4194320 | tf_op jit(solution)/shard_map/all_gather | solution.py:253
  473.1 13.3 %fusion.94 = (f32[2048]{0:T(1024)}, bf16[1024,2048]{1,0:T(8,128)(2,1)S(1)}) fusion(f32[1024,2048]{1,0:T(8,128)} %fusion.95, f32[2048]{0:T(1024)S(1)} %copy-done.64, bf16[1024,1024]{1,0:T(8,128)(2,1)} %all-gather.21.cloned.1.call-done, bf16[2048,1024]{0,1:T(8,128)(2,1)} %all-gather.19.cloned.1.call-done), kind=kOutput, calls=%fused_computation.166 | convolution fusion | flops 4339005440 | bytes 18890752 | tf_op jit(solution)/shard_map/dot_general | solution.py:60
  494.1 11.2 %convolution_convert_fusion.1 = bf16[1024,1024]{1,0:T(8,128)(2,1)} fusion(bf16[2048,1024]{0,1:T(8,128)(2,1)} %all-gather.19.cloned.1.call-done, f32[1024,2048]{1,0:T(8,128)} %fusion.95, f32[2048]{0:T(1024)S(1)} %copy-done.64), kind=kOutput, calls=%fused_computation.73 | convolution fusion | flops 4316987392 | bytes 14688256 | tf_op jit(solution)/shard_map/dot_general | solution.py:288
  505.6 19.1 %reduce-scatter.13.cloned.1.call-done = bf16[512,1024]{1,0:T(8,128)(2,1)} async-done(((bf16[1024,1024]{1,0:T(8,128)(2,1)}), bf16[512,1024]{1,0:T(8,128)(2,1)}) %reduce-scatter.13.cloned.1.call-update) | async-done | bytes 1048592 | tf_op jit(solution)/shard_map/reduce_scatter | solution.py:303
  527.5 31.3 %reduce-scatter.11.cloned.1.call-done = bf16[512,1024]{1,0:T(8,128)(2,1)} async-done(((bf16[1024,1024]{1,0:T(8,128)(2,1)}), bf16[512,1024]{1,0:T(8,128)(2,1)}) %reduce-scatter.11.cloned.1.call-update) | async-done | bytes 1048592 | tf_op jit(solution)/shard_map/reduce_scatter | solution.py:287
  566.1 33.2 %all-gather.23.cloned.1.call-done = bf16[1024,1024]{1,0:T(8,128)(2,1)} async-done(((bf16[512,1024]{1,0:T(8,128)(2,1)}), bf16[1024,1024]{1,0:T(8,128)(2,1)}) %all-gather.23.cloned.1.call-update) | async-done | bytes 2097168 | tf_op jit(solution)/shard_map/all_gather | solution.py:315
  603.1 14.2 %multiply_reduce_fusion.1 = (f32[8,512]{1,0:T(8,128)S(1)}, f32[8,512,1024]{2,1,0:T(8,128)}) fusion(f32[8,512,1024]{2,1,0:T(8,128)} %copy-done.1, f32[8,512]{1,0:T(8,128)S(1)} %log_add_fusion.1, bf16[512,8,64]{0,2,1:T(8,128)(2,1)S(1)} %bitcast.112, bf16[1024,8,3,64]{0,3,2,1:T(8,128)(2,1)} %bitcast.103), kind=kOutput, calls=%fused_computation.3 | convolution fusion | flops 549449728 | bytes 35160064 | tf_op jit(solution)/shard_map/qhd,khd->hqk/dot_general | solution.py:132
  638.7 14.9 %multiply_reduce_fusion = (f32[8,512]{1,0:T(8,128)}, f32[8,512,1024]{2,1,0:T(8,128)}) fusion(f32[8,512,1024]{2,1,0:T(8,128)} %copy-done, f32[8,512]{1,0:T(8,128)} %copy-done.35, bf16[512,8,64]{0,2,1:T(8,128)(2,1)} %bitcast.114, bf16[1024,8,3,64]{0,3,2,1:T(8,128)(2,1)} %bitcast.106), kind=kOutput, calls=%fused_computation.1 | convolution fusion | flops 549449728 | bytes 35160064 | tf_op jit(solution)/shard_map/qhd,khd->hqk/dot_general | solution.py:132
  676.4 9.1 fusion.93
  694.0 9.0 fusion.32
  716.4 17.0 %reduce-scatter.15.cloned.1.call-done = bf16[512,1024]{1,0:T(8,128)(2,1)} async-done(((bf16[1024,1024]{1,0:T(8,128)(2,1)}), bf16[512,1024]{1,0:T(8,128)(2,1)}) %reduce-scatter.15.cloned.1.call-update) | async-done | bytes 1048592 | tf_op jit(solution)/shard_map/reduce_scatter | solution.py:324
  735.7 40.3 %all-reduce = (f32[2048]{0:T(1024)S(1)}, f32[1024]{0:T(1024)S(1)}, f32[4096]{0:T(1024)S(1)}, f32[1024]{0:T(1024)S(1)}, f32[1024]{0:T(1024)S(1)}, /*index=5*/f32[...) all-reduce(f32[2048]{0:T(1024)S(1)} %dynamic_update_slice.6, ...), channel_id=1, replica_groups=mesh['dp'=16,'tensor'=2] {'dp','tensor'}, use_global_device_ids=true, to_apply=%region_20.21 | all-reduce | flops 12288 | bytes 98304 | tf_op jit(solution)/shard_map/psum | solution.py:347
  784.9 56.5 %reduce-scatter.21.cloned.1.call-done = f32[64,2048]{1,0:T(8,128)} async-done(((f32[1024,2048]{1,0:T(8,128)}), f32[64,2048]{1,0:T(8,128)}) %reduce-scatter.21.cloned.1.call-update) | async-done | bytes 524304 | tf_op jit(solution)/shard_map/reduce_scatter | solution.py:336
  844.3 86.2 %reduce-scatter.17.cloned.1.call-done = f32[64,1536]{1,0:T(8,128)} async-done(((f32[1024,1536]{1,0:T(8,128)}), f32[64,1536]{1,0:T(8,128)}) %reduce-scatter.17.cloned.1.call-update) | async-done | bytes 393232 | tf_op jit(solution)/shard_map/reduce_scatter | solution.py:334
  (321 shorter events, 172.7 us)
Async XLA Ops:
  7.3 40.7 %all-gather.9.cloned.1.call-start = ((), (), s32[]{:S(2)}) async-start(), calls=%async_computation.8 | async-start | bytes 3145728 | tf_op jit(solution)/shard_map/all_gather | solution.py:262
  12.0 84.3 %all-gather.11.cloned.1.call-start = ((), (), s32[]{:S(2)}) async-start(), calls=%async_computation.9 | async-start | bytes 3342336 | tf_op jit(solution)/shard_map/all_gather | solution.py:250
  12.8 135.9 %all-gather.13.cloned.1.call-start = ((), (), s32[]{:S(2)}) async-start(), calls=%async_computation.10 | async-start | bytes 1114112 | tf_op jit(solution)/shard_map/all_gather | solution.py:251
  13.6 169.8 %reduce-scatter.9.cloned.1.call-start = ((), (), s32[]{:S(2)}) async-start(), calls=%async_computation.11 | async-start | bytes 3145728 | tf_op jit(solution)/shard_map/reduce_scatter | solution.py:270
  133.2 484.0 %copy-start.33 = (f32[8,512]{1,0:T(8,128)}, f32[8,512]{1,0:T(8,128)S(1)}, u32[]{:S(2)}) copy-start(f32[8,512]{1,0:T(8,128)S(1)} %log_add_fusion.1) | copy-start | bytes 49156
  152.8 83.5 %all-gather.17.cloned.1.call-start = ((), (), s32[]{:S(2)}) async-start(), calls=%async_computation.13 | async-start | bytes 4456448 | tf_op jit(solution)/shard_map/all_gather | solution.py:252
  153.7 116.3 %all-gather.15.cloned.1.call-start = ((), (), s32[]{:S(2)}) async-start(), calls=%async_computation.12 | async-start | bytes 3145728 | tf_op jit(solution)/shard_map/all_gather | solution.py:281
  187.7 117.0 %all-gather.21.cloned.1.call-start = ((), (), s32[]{:S(2)}) async-start(), calls=%async_computation.16 | async-start | bytes 3145728 | tf_op jit(solution)/shard_map/all_gather | solution.py:295
  189.5 115.1 %copy-start.64 = (f32[2048]{0:T(1024)S(1)}, f32[2048]{0:T(1024)}, u32[]{:S(2)}) copy-start(f32[2048]{0:T(1024)} %param.47) | copy-start | bytes 24580
  189.5 230.8 %reduce-scatter.23.cloned.1.call-start = ((), (), s32[]{:S(2)}) async-start(), calls=%async_computation.23 | async-start | bytes 8912896 | tf_op jit(solution)/shard_map/reduce_scatter | solution.py:337
  316.7 103.6 %copy-start.25 = (f32[2048,64]{0,1:T(8,128)S(1)}, f32[2048,64]{0,1:T(8,128)}, u32[]{:S(2)}) copy-start(f32[2048,64]{0,1:T(8,128)} %param.48) | copy-start | bytes 1572868
  316.7 103.6 %copy-start.26 = (f32[2048,64]{0,1:T(8,128)S(1)}, f32[2048,64]{0,1:T(8,128)}, u32[]{:S(2)}) copy-start(f32[2048,64]{0,1:T(8,128)} %param.60) | copy-start | bytes 1572868
  316.7 103.6 %copy-start.27 = (f32[2048,64]{0,1:T(8,128)S(1)}, f32[2048,64]{0,1:T(8,128)}, u32[]{:S(2)}) copy-start(f32[2048,64]{0,1:T(8,128)} %param.72) | copy-start | bytes 1572868
  316.7 156.4 %all-gather.19.cloned.1.call-start = ((), (), s32[]{:S(2)}) async-start(), calls=%async_computation.14 | async-start | bytes 4456448 | tf_op jit(solution)/shard_map/all_gather | solution.py:253
  422.9 101.8 %reduce-scatter.13.cloned.1.call-start = ((), (), s32[]{:S(2)}) async-start(), calls=%async_computation.17 | async-start | bytes 3145728 | tf_op jit(solution)/shard_map/reduce_scatter | solution.py:303
  494.1 64.8 %reduce-scatter.11.cloned.1.call-start = ((), (), s32[]{:S(2)}) async-start(), calls=%async_computation.15 | async-start | bytes 3145728 | tf_op jit(solution)/shard_map/reduce_scatter | solution.py:287
  505.4 93.9 %all-gather.23.cloned.1.call-start = ((), (), s32[]{:S(2)}) async-start(), calls=%async_computation.18 | async-start | bytes 3145728 | tf_op jit(solution)/shard_map/all_gather | solution.py:315
  566.1 148.6 %reduce-scatter.19.cloned.1.call-start = ((), (), s32[]{:S(2)}) async-start(), calls=%async_computation.21 | async-start | bytes 2228224 | tf_op jit(solution)/shard_map/reduce_scatter | solution.py:335
  638.4 95.0 %reduce-scatter.15.cloned.1.call-start = ((), (), s32[]{:S(2)}) async-start(), calls=%async_computation.19 | async-start | bytes 3145728 | tf_op jit(solution)/shard_map/reduce_scatter | solution.py:324
  693.7 147.7 %reduce-scatter.21.cloned.1.call-start = ((), (), s32[]{:S(2)}) async-start(), calls=%async_computation.22 | async-start | bytes 8912896 | tf_op jit(solution)/shard_map/reduce_scatter | solution.py:336
  703.0 227.4 %reduce-scatter.17.cloned.1.call-start = ((), (), s32[]{:S(2)}) async-start(), calls=%async_computation.20 | async-start | bytes 6684672 | tf_op jit(solution)/shard_map/reduce_scatter | solution.py:334
  784.9 145.6 %copy-start.24 = (f32[64,1536]{1,0:T(8,128)S(1)}, f32[64,1536]{1,0:T(8,128)}, u32[]{:S(2)}) copy-start(f32[64,1536]{1,0:T(8,128)} %param.42) | copy-start | bytes 1179652
  784.9 145.6 %copy-start.37 = (f32[64,1536]{1,0:T(8,128)S(1)}, f32[64,1536]{1,0:T(8,128)}, u32[]{:S(2)}) copy-start(f32[64,1536]{1,0:T(8,128)} %param.54) | copy-start | bytes 1179652
  784.9 145.6 %copy-start.38 = (f32[64,1536]{1,0:T(8,128)S(1)}, f32[64,1536]{1,0:T(8,128)}, u32[]{:S(2)}) copy-start(f32[64,1536]{1,0:T(8,128)} %param.66) | copy-start | bytes 1179652
  (95 other events, 2160.3 us)
Sparse Core Ops, SparseCore 0:
  12.2 35.8 all-gather.8
  50.9 45.4 all-gather.10
  99.1 36.1 all-gather.12
  152.9 30.3 reduce-scatter.8
  185.9 50.3 all-gather.16
  238.3 31.6 all-gather.14
  271.5 33.0 all-gather.20
  316.8 103.4 reduce-scatter.22
  423.0 50.0 all-gather.18
  494.2 30.4 reduce-scatter.12
  526.9 31.8 reduce-scatter.10
  566.2 33.0 all-gather.22
  638.5 61.9 reduce-scatter.18
  702.5 30.8 reduce-scatter.14
  737.9 103.4 reduce-scatter.20
  845.8 84.6 reduce-scatter.16
where the time goes:
time: 948 us; the launch traced here: 940 us
  waiting for transfers between devices  609 us (64%)
  matrix products  175 us (18%)
  other arithmetic  68.7 us (7%)
  blocking collectives  40.3 us (4%)
  local copies, waits for them, and re-layouts  29.4 us (3%)
  between operations  15.5 us (2%)
    reduce_scatter x1, waiting for transfers between devices, local(): lax.psum_scatter(contraction_sensitivity, 'dp', scatter_dimension=1, tile...  104 us
    reduce_scatter x1, waiting for transfers between devices, local(): lax.psum_scatter(packed_triple_slope, 'dp', scatter_dimension=0, tiled=True)  86.2 us
    reduce_scatter x1, waiting for transfers between devices, local(): lax.psum_scatter(expansion_sensitivity, 'dp', scatter_dimension=0, tiled=...  56.5 us
    all_gather x1, waiting for transfers between devices, local(): lax.all_gather(down_weight.astype(jnp.bfloat16), 'dp', axis=1, tiled=True)  49.8 us
    all_gather x1, waiting for transfers between devices, local(): lax.all_gather(qkv_weight.astype(jnp.bfloat16), 'dp', axis=0, tiled=True)  48.4 us
    all_gather x1, waiting for transfers between devices, local(): lax.all_gather(up_weight.astype(jnp.bfloat16), 'dp', axis=0, tiled=True)  46.6 us
    psum x1, blocking collectives, local(): lax.psum((jnp.sum(skip_path_sensitivity, axis=0), jnp.sum(leaving_activat...  40.3 us
    all_gather x1, waiting for transfers between devices, local(): lax.all_gather(perceptron_standardised, 'tensor', axis=0, tiled=True)  33.6 us
  transfers between devices with their start and end apart: 16, of which 14 were waited for; matrix products, arithmetic and copies ran while one was open for 18% of the time, Pallas kernels for 0%

commit v1 on v0

v1 whole, which is shorter than its diff:
```python
import functools

import jax
import jax.numpy as jnp
from jax import lax
from jax.experimental import pallas as pl
from jax.experimental.pallas import tpu as pltpu
from jax.sharding import PartitionSpec as P

D = 1024
FOCUS_COUNT = 16
FF = 4096
ADAM_STEP = 4
HEAD_DIM = 64
MAX_SPAN = 512


beta_first = 0.9
beta_second = 0.95


def standardise_features(values, elementwise_multiplier, additive_offset):
    feature_midpoint = jnp.mean(values, axis=-1, keepdims=True)
    demeaned_entries = values - feature_midpoint
    reciprocal_spread = lax.rsqrt(
        jnp.mean(demeaned_entries * demeaned_entries, axis=-1, keepdims=True) + 1e-05
    )
    unit_spread_entries = demeaned_entries * reciprocal_spread
    return (
        (unit_spread_entries * elementwise_multiplier + additive_offset).astype(jnp.bfloat16),
        unit_spread_entries,
        reciprocal_spread,
    )


def standardise_features_reverse(
    loss_slope, unit_spread_entries, reciprocal_spread, elementwise_multiplier
):
    multiplied_entries = loss_slope * elementwise_multiplier
    return reciprocal_spread * (
        multiplied_entries
        - jnp.mean(multiplied_entries, axis=-1, keepdims=True)
        - unit_spread_entries
        * jnp.mean(multiplied_entries * unit_spread_entries, axis=-1, keepdims=True)
    )


def gelu_parts(pre):
    inner = 0.7978845608 * (pre + 0.044715 * pre * pre * pre)
    tanh_val = jnp.tanh(inner)
    value = 0.5 * pre * (1.0 + tanh_val)
    slope = 0.5 * (1.0 + tanh_val) + 0.5 * pre * (1.0 - tanh_val * tanh_val) * 0.7978845608 * (
        1.0 + 3.0 * 0.044715 * pre * pre
    )
    return (value, slope)


def inner_rows(left, right):
    return lax.dot_general(
        left, right, (((0,), (0,)), ((), ())), preferred_element_type=jnp.float32
    )


def times_transposed(left, right):
    return lax.dot_general(
        left, right, (((1,), (1,)), ((), ())), preferred_element_type=jnp.float32
    )


def head_slopes(first, count):
    index = (first + jnp.arange(count)).astype(jnp.float32)
    return jnp.exp2(-8.0 * (index + 1.0) / FOCUS_COUNT)


def full_bias(qv_bias, heads):
    pair = qv_bias.reshape(heads, 2, HEAD_DIM)
    return jnp.stack([pair[:, 0], jnp.zeros_like(pair[:, 0]), pair[:, 1]], axis=1).reshape(
        heads * 3 * HEAD_DIM
    )


def window(start, block, length):
    return (max(0, start - MAX_SPAN), min(length, start + block))


def fill_offsets(offsets, rows_seg, cols_seg, rows_first, length, block):
    for start in range(0, length, block):
        low, high = window(start, block, length)
        shape = (block, high - low) if rows_first else (high - low, block)
        axis = 0 if rows_first else 1
        row = start + lax.broadcasted_iota(jnp.int32, shape, axis)
        col = low + lax.broadcasted_iota(jnp.int32, shape, 1 - axis)
        if rows_first:
            same = rows_seg[start : start + block, :] == cols_seg[:, low:high]
        else:
            same = rows_seg[low:high, :] == cols_seg[:, start : start + block]
        allowed = (col <= row) & same
        value = jnp.where(allowed, (col - row).astype(jnp.float32), -1e30)
        if rows_first:
            offsets[start : start + block, 0 : high - low] = value
        else:
            offsets[0 : high - low, start : start + block] = value


def forward_kernel(block, slopes, x, rows_seg, cols_seg, out, offsets):
    length = x.shape[0]
    step = pl.program_id(0)

    @pl.when(step == 0)
    def _():
        fill_offsets(offsets, rows_seg, cols_seg, True, length, block)

    for i in range(2):
        base = 3 * HEAD_DIM * i
        slope = slopes[2 * step + i]
        query = x[:, base : base + HEAD_DIM] * HEAD_DIM ** (-0.5)
        keys = x[:, base + HEAD_DIM : base + 2 * HEAD_DIM]
        values = x[:, base + 2 * HEAD_DIM : base + 3 * HEAD_DIM]
        for start in range(0, length, block):
            low, high = window(start, block, length)
            scores = (
                times_transposed(query[start : start + block], keys[low:high])
                + slope * offsets[start : start + block, 0 : high - low]
            )
            peak = jnp.max(scores, axis=1, keepdims=True)
            raised = jnp.exp(scores - peak)
            total = jnp.sum(raised, axis=1, keepdims=True)
            probs = (raised * (1.0 / total)).astype(jnp.bfloat16)
            context = jnp.dot(probs, values[low:high], preferred_element_type=jnp.float32)
            out[start : start + block, HEAD_DIM * i : HEAD_DIM * (i + 1)] = context.astype(
                jnp.bfloat16
            )


def backward_kernel(
    block, slopes, x, grad, rows_seg, cols_seg, out, sums, offsets, dkeys, dvalues, dquery
):
    length = x.shape[0]
    step = pl.program_id(0)
    scale = HEAD_DIM ** (-0.5)

    @pl.when(step == 0)
    def _():
        fill_offsets(offsets, rows_seg, cols_seg, False, length, block)

    for i in range(2):
        base = 3 * HEAD_DIM * i
        slope = slopes[2 * step + i]
        query = x[:, base : base + HEAD_DIM] * scale
        keys = x[:, base + HEAD_DIM : base + 2 * HEAD_DIM]
        values = x[:, base + 2 * HEAD_DIM : base + 3 * HEAD_DIM]
        slopes_out = grad[:, HEAD_DIM * i : HEAD_DIM * (i + 1)]
        dkeys[...] = jnp.zeros_like(dkeys)
        dvalues[...] = jnp.zeros_like(dvalues)
        for start in range(0, length, block):
            low, high = window(start, block, length)
            query_block = query[start : start + block]
            grad_block = slopes_out[start : start + block]
            scores = (
                times_transposed(keys[low:high], query_block)
                + slope * offsets[0 : high - low, start : start + block]
            )
            peak = jnp.max(scores, axis=0, keepdims=True)
            raised = jnp.exp(scores - peak)
            total = jnp.sum(raised, axis=0, keepdims=True)
            probs = raised * (1.0 / total)
            dprob = times_transposed(values[low:high], grad_block)
            delta = jnp.sum(probs * dprob, axis=0, keepdims=True)
            dscore = (probs * (dprob - delta)).astype(jnp.bfloat16)
            dvalues[low:high, :] += jnp.dot(
                probs.astype(jnp.bfloat16), grad_block, preferred_element_type=jnp.float32
            )
            dkeys[low:high, :] += jnp.dot(dscore, query_block, preferred_element_type=jnp.float32)
            dquery[start : start + block, :] = inner_rows(dscore, keys[low:high]) * scale
        for place, part in enumerate((dquery, dkeys, dvalues)):
            first = base + HEAD_DIM * place
            out[:, first : first + HEAD_DIM] = part[...].astype(jnp.bfloat16)
            sums[:, first : first + HEAD_DIM] = jnp.sum(part[...], axis=0, keepdims=True)


def attention_forward(qkv, segments, slopes):
    length, width = qkv.shape
    pairs = width // (6 * HEAD_DIM)
    block = min(256, length)
    span = min(length, block + MAX_SPAN)
    return pl.pallas_call(
        functools.partial(forward_kernel, block),
        grid=(pairs,),
        out_shape=jax.ShapeDtypeStruct((length, width // 3), jnp.bfloat16),
        in_specs=[
            pl.BlockSpec(memory_space=pltpu.SMEM),
            pl.BlockSpec((length, 6 * HEAD_DIM), lambda p: (0, p)),
            pl.BlockSpec((length, 1), lambda p: (0, 0)),
            pl.BlockSpec((1, length), lambda p: (0, 0)),
        ],
        out_specs=pl.BlockSpec((length, 2 * HEAD_DIM), lambda p: (0, p)),
        scratch_shapes=[pltpu.VMEM((length, span), jnp.float32)],
        cost_estimate=pl.CostEstimate(
            flops=4 * length * span * width // 3,
            bytes_accessed=8 * length * width // 3,
            transcendentals=length * span * pairs * 2,
        ),
        compiler_params=pltpu.CompilerParams(vmem_limit_bytes=40 * 1024 * 1024),
        name="attention_forward",
    )(slopes, qkv, segments[:, None], segments[None, :])


def attention_backward(qkv, segments, slopes, dcontext):
    length, width = qkv.shape
    pairs = width // (6 * HEAD_DIM)
    block = min(256, length)
    span = min(length, block + MAX_SPAN)
    return pl.pallas_call(
        functools.partial(backward_kernel, block),
        grid=(pairs,),
        out_shape=(
            jax.ShapeDtypeStruct((length, width), jnp.bfloat16),
            jax.ShapeDtypeStruct((1, width), jnp.float32),
        ),
        in_specs=[
            pl.BlockSpec(memory_space=pltpu.SMEM),
            pl.BlockSpec((length, 6 * HEAD_DIM), lambda p: (0, p)),
            pl.BlockSpec((length, 2 * HEAD_DIM), lambda p: (0, p)),
            pl.BlockSpec((length, 1), lambda p: (0, 0)),
            pl.BlockSpec((1, length), lambda p: (0, 0)),
        ],
        out_specs=(
            pl.BlockSpec((length, 6 * HEAD_DIM), lambda p: (0, p)),
            pl.BlockSpec((1, 6 * HEAD_DIM), lambda p: (0, p)),
        ),
        scratch_shapes=[
            pltpu.VMEM((span, length), jnp.float32),
            pltpu.VMEM((length, HEAD_DIM), jnp.float32),
            pltpu.VMEM((length, HEAD_DIM), jnp.float32),
            pltpu.VMEM((length, HEAD_DIM), jnp.float32),
        ],
        cost_estimate=pl.CostEstimate(
            flops=10 * length * span * width // 3,
            bytes_accessed=14 * length * width // 3,
            transcendentals=length * span * pairs * 2,
        ),
        compiler_params=pltpu.CompilerParams(vmem_limit_bytes=40 * 1024 * 1024),
        name="attention_backward",
    )(slopes, qkv, dcontext, segments[:, None], segments[None, :])


def swap(values):
    return lax.ppermute(values, "tensor", [(0, 1), (1, 0)])


def spread(values, count):
    if count == 2:
        return [values, swap(values)]
    return [lax.all_gather(values, "tensor", axis=0, tiled=True)]


def fold(parts, count):
    if count == 2:
        return swap(parts[1]).astype(jnp.float32) + parts[0].astype(jnp.float32)
    return lax.psum_scatter(parts[0], "tensor", scatter_dimension=0, tiled=True).astype(
        jnp.float32
    )


def to_order(parts, rank):
    if len(parts) == 2:
        own, other = parts
        return jnp.concatenate(
            [jnp.where(rank == 0, own, other), jnp.where(rank == 0, other, own)], axis=0
        )
    return parts[0]


def from_order(values, rank, count):
    if count == 2:
        half = values.shape[0] // 2
        return [
            lax.dynamic_slice_in_dim(values, rank * half, half, 0),
            lax.dynamic_slice_in_dim(values, (1 - rank) * half, half, 0),
        ]
    return [values]


def product(left, right):
    return jnp.dot(left, right, preferred_element_type=jnp.float32)


def add_up(lefts, rights):
    total = inner_rows(lefts[0], rights[0])
    for left, right in zip(lefts[1:], rights[1:]):
        total = total + inner_rows(left, right)
    return total


def total_over_all(vector, shared, rank):
    rows = lax.all_gather(vector[None], ("dp", "tensor"), axis=0, tiled=True)
    everyone = jnp.sum(rows[:, :shared], axis=0)
    count = lax.axis_size("tensor")
    split = rows[:, shared:].reshape(rows.shape[0] // count, count, -1)
    mine = lax.dynamic_index_in_dim(jnp.sum(split, axis=0), rank, 0, keepdims=False)
    return everyone, mine


def adamw(param, loss_slope, first, second, rate, decay):
    first_new = beta_first * first + (1.0 - beta_first) * loss_slope
    second_new = beta_second * second + (1.0 - beta_second) * loss_slope * loss_slope
    update = (
        first_new
        / (1.0 - beta_first**ADAM_STEP)
        / (jnp.sqrt(second_new / (1.0 - beta_second**ADAM_STEP)) + 1e-08)
    )
    return (param - rate * (update + decay * param), first_new, second_new)


def local(
    entering_activations,
    segment_ids,
    leaving_activation_slope,
    qkv_weight,
    qv_bias,
    dense_weight,
    dense_bias,
    up_weight,
    up_bias,
    down_weight,
    down_bias,
    mixer_scale_factor,
    mixer_offset_term,
    perceptron_scale_factor,
    perceptron_offset_term,
    first_qkv_weight,
    first_qv_bias,
    first_dense_weight,
    first_dense_bias,
    first_up_weight,
    first_up_bias,
    first_down_weight,
    first_down_bias,
    first_norm1_gain,
    first_norm1_bias,
    first_norm2_gain,
    first_norm2_bias,
    second_qkv_weight,
    second_qv_bias,
    second_dense_weight,
    second_dense_bias,
    second_up_weight,
    second_up_bias,
    second_down_weight,
    second_down_bias,
    second_norm1_gain,
    second_norm1_bias,
    second_norm2_gain,
    second_norm2_bias,
):
    params = (
        qkv_weight,
        qv_bias,
        dense_weight,
        dense_bias,
        up_weight,
        up_bias,
        down_weight,
        down_bias,
        mixer_scale_factor,
        mixer_offset_term,
        perceptron_scale_factor,
        perceptron_offset_term,
    )
    firsts = (
        first_qkv_weight,
        first_qv_bias,
        first_dense_weight,
        first_dense_bias,
        first_up_weight,
        first_up_bias,
        first_down_weight,
        first_down_bias,
        first_norm1_gain,
        first_norm1_bias,
        first_norm2_gain,
        first_norm2_bias,
    )
    seconds = (
        second_qkv_weight,
        second_qv_bias,
        second_dense_weight,
        second_dense_bias,
        second_up_weight,
        second_up_bias,
        second_down_weight,
        second_down_bias,
        second_norm1_gain,
        second_norm1_bias,
        second_norm2_gain,
        second_norm2_bias,
    )
    qkv_low, dense_low, up_low, down_low = (
        lax.all_gather(qkv_weight.astype(jnp.bfloat16), "dp", axis=0, tiled=True),
        lax.all_gather(dense_weight.astype(jnp.bfloat16), "dp", axis=1, tiled=True),
        lax.all_gather(up_weight.astype(jnp.bfloat16), "dp", axis=0, tiled=True),
        lax.all_gather(down_weight.astype(jnp.bfloat16), "dp", axis=1, tiled=True),
    )
    local_heads = qkv_low.shape[1] // (3 * HEAD_DIM)
    tensor_rank = lax.axis_index("tensor")
    count = lax.axis_size("tensor")
    slopes = head_slopes(tensor_rank * local_heads, local_heads)
    segments = segment_ids[0]
    mixer_standardised, mixer_unit_spread1, mixer_reciprocal_spread1 = standardise_features(
        entering_activations, mixer_scale_factor, mixer_offset_term
    )
    ones = spread(mixer_standardised, count)
    outs = spread(leaving_activation_slope.astype(jnp.bfloat16), count)
    qkv_bias = full_bias(qv_bias, local_heads)
    qkv = to_order([(product(one, qkv_low) + qkv_bias).astype(jnp.bfloat16) for one in ones], tensor_rank)
    context = attention_forward(qkv, segments, slopes)
    contexts = from_order(context, tensor_rank, count)
    skip_path_sum = (
        entering_activations
        + fold([product(part, dense_low).astype(jnp.bfloat16) for part in contexts], count)
        + dense_bias
    )
    perceptron_standardised, perceptron_unit_spread2, perceptron_reciprocal_spread2 = (
        standardise_features(skip_path_sum, perceptron_scale_factor, perceptron_offset_term)
    )
    twos = spread(perceptron_standardised, count)
    acts, dpres, dpre_lows, pre_parts = [], [], [], []
    for two, out in zip(twos, outs):
        act_val, act_slope = gelu_parts(product(two, up_low) + up_bias)
        acts.append(act_val.astype(jnp.bfloat16))
        dpres.append(times_transposed(out, down_low) * act_slope)
        dpre_lows.append(dpres[-1].astype(jnp.bfloat16))
        pre_parts.append(times_transposed(dpre_lows[-1], up_low).astype(jnp.bfloat16))
    pre_perceptron_sensitivity = fold(pre_parts, count)
    block_out = (
        skip_path_sum
        + fold([product(act, down_low).astype(jnp.bfloat16) for act in acts], count)
        + down_bias
    )
    contraction_sensitivity = add_up(acts, outs).astype(jnp.bfloat16)
    expansion_sensitivity = add_up(twos, dpre_lows).astype(jnp.bfloat16)
    up_bias_part = sum(jnp.sum(dpre, axis=0) for dpre in dpres)
    skip_path_sensitivity = leaving_activation_slope + standardise_features_reverse(
        pre_perceptron_sensitivity,
        perceptron_unit_spread2,
        perceptron_reciprocal_spread2,
        perceptron_scale_factor,
    )
    resids = spread(skip_path_sensitivity.astype(jnp.bfloat16), count)
    mixer_merge_sensitivity = add_up(contexts, resids).astype(jnp.bfloat16)
    dcontext = to_order(
        [times_transposed(resid, dense_low).astype(jnp.bfloat16) for resid in resids], tensor_rank
    )
    dqkv_low, dqkv_sums = attention_backward(qkv, segments, slopes, dcontext)
    dqkv_lows = from_order(dqkv_low, tensor_rank, count)
    packed_triple_slope = add_up(ones, dqkv_lows).astype(jnp.bfloat16)
    triple = dqkv_sums.reshape(local_heads, 3, HEAD_DIM)
    qv_part = jnp.stack([triple[:, 0], triple[:, 2]], axis=1).reshape(-1)
    pre_mixer_sensitivity = fold(
        [times_transposed(part, qkv_low).astype(jnp.bfloat16) for part in dqkv_lows], count
    )
    entering_activation_slope = skip_path_sensitivity + standardise_features_reverse(
        pre_mixer_sensitivity, mixer_unit_spread1, mixer_reciprocal_spread1, mixer_scale_factor
    )
    early, up_bias_grad = total_over_all(
        jnp.concatenate(
            [
                jnp.sum(skip_path_sensitivity, axis=0),
                jnp.sum(leaving_activation_slope, axis=0),
                jnp.sum(pre_perceptron_sensitivity * perceptron_unit_spread2, axis=0),
                jnp.sum(pre_perceptron_sensitivity, axis=0),
                up_bias_part,
            ]
        ),
        4 * D,
        tensor_rank,
    )
    dense_bias_grad, down_bias_grad, gain_two_grad, shift_two_grad = jnp.split(early, 4)
    late, qv_bias_grad = total_over_all(
        jnp.concatenate(
            [
                jnp.sum(pre_mixer_sensitivity * mixer_unit_spread1, axis=0),
                jnp.sum(pre_mixer_sensitivity, axis=0),
                qv_part,
            ]
        ),
        2 * D,
        tensor_rank,
    )
    gain_one_grad, shift_one_grad = jnp.split(late, 2)
    packed_triple_slope, mixer_merge_sensitivity, expansion_sensitivity, contraction_sensitivity = (
        part.astype(jnp.float32)
        for part in (
            lax.psum_scatter(packed_triple_slope, "dp", scatter_dimension=0, tiled=True),
            lax.psum_scatter(mixer_merge_sensitivity, "dp", scatter_dimension=1, tiled=True),
            lax.psum_scatter(expansion_sensitivity, "dp", scatter_dimension=0, tiled=True),
            lax.psum_scatter(contraction_sensitivity, "dp", scatter_dimension=1, tiled=True),
        )
    )
    parameter_slopes = (
        packed_triple_slope,
        qv_bias_grad,
        mixer_merge_sensitivity,
        dense_bias_grad,
        expansion_sensitivity,
        up_bias_grad,
        contraction_sensitivity,
        down_bias_grad,
        gain_one_grad,
        shift_one_grad,
        gain_two_grad,
        shift_two_grad,
    )
    results = []
    for index in range(12):
        matrix = index in (0, 2, 4, 6)
        results.append(
            adamw(
                params[index],
                parameter_slopes[index],
                firsts[index],
                seconds[index],
                0.01 if matrix else 0.1,
                0.1 if matrix else 0.0,
            )
        )
    news = [r[0] for r in results]
    moments_one = [r[1] for r in results]
    moments_two = [r[2] for r in results]
    return (
        block_out,
        entering_activation_slope,
        *parameter_slopes,
        *news,
        *moments_one,
        *moments_two,
    )


def solution(mesh):
    in_specs = (
        P(("dp", "tensor"), None),
        P("dp", None),
        P(("dp", "tensor"), None),
        P("dp", "tensor"),
        P("tensor"),
        P("tensor", "dp"),
        P(),
        P("dp", "tensor"),
        P("tensor"),
        P("tensor", "dp"),
        P(),
        P(),
        P(),
        P(),
        P(),
        P("dp", "tensor"),
        P("tensor"),
        P("tensor", "dp"),
        P(),
        P("dp", "tensor"),
        P("tensor"),
        P("tensor", "dp"),
        P(),
        P(),
        P(),
        P(),
        P(),
        P("dp", "tensor"),
        P("tensor"),
        P("tensor", "dp"),
        P(),
        P("dp", "tensor"),
        P("tensor"),
        P("tensor", "dp"),
        P(),
        P(),
        P(),
        P(),
        P(),
    )
    out_specs = (
        P(("dp", "tensor"), None),
        P(("dp", "tensor"), None),
        P("dp", "tensor"),
        P("tensor"),
        P("tensor", "dp"),
        P(),
        P("dp", "tensor"),
        P("tensor"),
        P("tensor", "dp"),
        P(),
        P(),
        P(),
        P(),
        P(),
        P("dp", "tensor"),
        P("tensor"),
        P("tensor", "dp"),
        P(),
        P("dp", "tensor"),
        P("tensor"),
        P("tensor", "dp"),
        P(),
        P(),
        P(),
        P(),
        P(),
        P("dp", "tensor"),
        P("tensor"),
        P("tensor", "dp"),
        P(),
        P("dp", "tensor"),
        P("tensor"),
        P("tensor", "dp"),
        P(),
        P(),
        P(),
        P(),
        P(),
        P("dp", "tensor"),
        P("tensor"),
        P("tensor", "dp"),
        P(),
        P("dp", "tensor"),
        P("tensor"),
        P("tensor", "dp"),
        P(),
        P(),
        P(),
        P(),
        P(),
    )
    return jax.shard_map(local, mesh=mesh, in_specs=in_specs, out_specs=out_specs, check_vma=False)
```

time: 948 us -> 662 us (0.70)
  waiting for transfers between devices: 609 us -> 281 us
  blocking collectives: 40.3 us -> 159 us
  matrix products: 175 us -> 96 us
  Pallas kernels: 0 us -> 45.1 us
  other arithmetic: 68.7 us -> 28.6 us
  local copies, waits for them, and re-layouts: 29.4 us -> 17.1 us
  starting transfers between devices: 1.92 us -> 12.1 us
    all_gather x0 -> x2, blocking collectives: none -> 159 us  [total_over_all(): rows = lax.all_gather(vector[None], ('dp', 'tensor'), axis=0, tiled=True)]
    all_gather x4 -> x0, waiting for transfers between devices: 120 us -> none  [the longest x1 33.6 us: local(): lax.all_gather(perceptron_standardised, 'tensor', axis=0, tiled=True)]
    reduce_scatter x4 -> x0, waiting for transfers between devices: 97 us -> none  [the longest x1 31.3 us: local(): lax.psum_scatter(jnp.dot(act, down_low, preferred_element_type=jnp.float3...]
    ppermute x0 -> x8, waiting for transfers between devices: none -> 90.7 us  [swap(): return lax.ppermute(values, 'tensor', [(0, 1), (1, 0)])]
    reduce_scatter x1, waiting for transfers between devices: 86.2 us -> 0.01 us  [local(): lax.psum_scatter(packed_triple_slope, 'dp', scatter_dimension=0, tiled=True)]
    dot_general x16 -> x8, matrix products: 118 us -> 33.4 us  [product(): return jnp.dot(left, right, preferred_element_type=jnp.float32)]
    reduce_scatter x1, waiting for transfers between devices: 56.5 us -> 0.01 us  [local(): lax.psum_scatter(expansion_sensitivity, 'dp', scatter_dimension=0, tiled=...]
    pallas_call x0 -> x2, Pallas kernels: none -> 45.1 us  [the longest x1 27.1 us: attention_backward(): pl.pallas_call(functools.partial(backward_kernel, block), grid=(pairs,),...]
  transfers between devices with their start and end apart: 16 -> 16, of which waited for: 14 -> 10; matrix products, arithmetic and copies ran while one was open for 18% -> 15% of each run, Pallas kernels for 0% -> 7%
where the time goes in v1:
time: 662 us; the launch traced here: 655 us
  waiting for transfers between devices  281 us (42%)
  blocking collectives  159 us (24%)
  matrix products  96 us (15%)
  Pallas kernels  45.1 us (7%)
  other arithmetic  28.6 us (4%)
  local copies, waits for them, and re-layouts  17.1 us (3%)
  between operations  15.6 us (2%)
  starting transfers between devices  12.1 us (2%)
    all_gather x2, blocking collectives, total_over_all(): rows = lax.all_gather(vector[None], ('dp', 'tensor'), axis=0, tiled=True)  159 us
    ppermute x8, waiting for transfers between devices, swap(): return lax.ppermute(values, 'tensor', [(0, 1), (1, 0)])  90.7 us
    reduce_scatter x1, waiting for transfers between devices, local(): lax.psum_scatter(contraction_sensitivity, 'dp', scatter_dimension=1, tile...  71.9 us
    all_gather x1, waiting for transfers between devices, local(): lax.all_gather(down_weight.astype(jnp.bfloat16), 'dp', axis=1, tiled=True)  49.1 us
    all_gather x1, waiting for transfers between devices, local(): lax.all_gather(qkv_weight.astype(jnp.bfloat16), 'dp', axis=0, tiled=True)  40.9 us
    dot_general x8, matrix products, times_transposed(): lax.dot_general(left, right, (((1,), (1,)), ((), ())), preferred_element_...  34 us
    dot_general x8, matrix products, product(): return jnp.dot(left, right, preferred_element_type=jnp.float32)  33.4 us
    dot_general x8, matrix products, inner_rows(): lax.dot_general(left, right, (((0,), (0,)), ((), ())), preferred_element_...  28.7 us
  transfers between devices with their start and end apart: 16, of which 10 were waited for; matrix products, arithmetic and copies ran while one was open for 15% of the time, Pallas kernels for 7%

profile of v1, /device:TPU:0, one launch (start us, length us, event | category | flops | bytes accessed | tf_op | source)
XLA Modules:
  0.0 654.8 jit_solution(17106622343729361962)
XLA Ops:
  18.1 40.9 %all-gather.7.cloned.1.call-done = bf16[1024,1536]{1,0:T(8,128)(2,1)} async-done(((bf16[64,1536]{1,0:T(8,128)(2,1)}), bf16[1024,1536]{1,0:T(8,128)(2,1)}) %all-gather.7.cloned.1.call-update) | async-done | bytes 3145744 | tf_op jit(solution)/shard_map/all_gather | solution.py:399
  65.8 18.0 %attention_forward.1 = bf16[1024,512]{1,0:T(8,128)(2,1)S(1)} custom-call(f32[8]{0:T(128)S(1)} %multiply_exponential_fusion.slopes, bf16[1024,1536]{1,0:T(8,128)(2,1)S(1)} %pad_maximum_fusion.x, s32[1024,1]{1,0:T(8,128)S(1)} %copy-done.2, s32[1,1024]{1,0:T(1,128)S(1)} %copy-done.4), custom_call_target="tpu_custom_call" | custom-call | flops 1610612736 | bytes 4194304 | tf_op jit(solution)/shard_map/attention_forward/pallas_call | solution.py:186
  84.7 13.3 %all-gather.9.cloned.1.call-done = bf16[512,1024]{0,1:T(8,128)(2,1)} async-done(((bf16[512,64]{0,1:T(8,128)(2,1)}), bf16[512,1024]{0,1:T(8,128)(2,1)}) %all-gather.9.cloned.1.call-update) | async-done | bytes 1048592 | tf_op jit(solution)/shard_map/all_gather | solution.py:400
  104.5 23.1 %collective-permute-done.1 = bf16[512,1024]{1,0:T(8,128)(2,1)} collective-permute-done((bf16[512,1024]{1,0:T(8,128)(2,1)}, bf16[512,1024]{1,0:T(8,128)(2,1)}, u32[]{:S(2)}, u32[]{:S(2)}) %collective-permute-start.1) | collective-permute-done | bytes 1048608 | tf_op jit(solution)/shard_map/ppermute | solution.py:248
  135.1 15.1 %all-gather.11.cloned.1.call-done = bf16[1024,2048]{1,0:T(8,128)(2,1)} async-done(((bf16[64,2048]{1,0:T(8,128)(2,1)}), bf16[1024,2048]{1,0:T(8,128)(2,1)}) %all-gather.11.cloned.1.call-update) | async-done | bytes 4194320 | tf_op jit(solution)/shard_map/all_gather | solution.py:401
  150.2 4.8 fusion.79
  155.1 4.8 fusion.58
  159.9 11.9 %collective-permute-done.2 = bf16[512,1024]{1,0:T(8,128)(2,1)} collective-permute-done((bf16[512,1024]{1,0:T(8,128)(2,1)}, bf16[512,1024]{1,0:T(8,128)(2,1)}, u32[]{:S(2)}, u32[]{:S(2)}) %collective-permute-start.2) | collective-permute-done | bytes 1048608 | tf_op jit(solution)/shard_map/ppermute | solution.py:248
  177.4 5.8 add_convert_fusion
  183.2 71.9 %reduce-scatter.11.cloned.1.call-done = bf16[2048,64]{0,1:T(8,128)(2,1)} async-done(((bf16[2048,1024]{0,1:T(8,128)(2,1)}), bf16[2048,64]{0,1:T(8,128)(2,1)}) %reduce-scatter.11.cloned.1.call-update) | async-done | bytes 262160 | tf_op jit(solution)/shard_map/reduce_scatter | solution.py:497
  258.7 49.1 %all-gather.13.cloned.1.call-done = bf16[2048,1024]{0,1:T(8,128)(2,1)} async-done(((bf16[2048,64]{0,1:T(8,128)(2,1)}), bf16[2048,1024]{0,1:T(8,128)(2,1)}) %all-gather.13.cloned.1.call-update) | async-done | bytes 4194320 | tf_op jit(solution)/shard_map/all_gather | solution.py:402
  307.8 8.4 %fusion.77 = (f32[2048]{0:T(1024)S(1)}, bf16[512,2048]{1,0:T(8,128)(2,1)S(1)}) fusion(f32[512,2048]{1,0:T(8,128)} %copy-done.64, f32[2048]{0:T(1024)S(1)} %copy-done.38, bf16[512,1024]{1,0:T(8,128)(2,1)} %collective-permute-done.4, bf16[2048,1024]{0,1:T(8,128)(2,1)} %all-gather.13.cloned.1.call-done), kind=kOutput, calls=%fused_computation.164 | convolution fusion | flops 2169501696 | bytes 11550720 | tf_op jit(solution)/shard_map/dot_general | solution.py:65
  321.5 6.2 fusion.76
  327.6 17.7 %collective-permute-done.5 = bf16[512,1024]{1,0:T(8,128)(2,1)S(1)} collective-permute-done((bf16[512,1024]{1,0:T(8,128)(2,1)S(1)}, bf16[512,1024]{1,0:T(8,128)(2,1)S(1)}, u32[]{:S(2)}, u32[]{:S(2)}) %collective-permute-start.5) | collective-permute-done | bytes 1048608 | tf_op jit(solution)/shard_map/ppermute | solution.py:248
  351.0 23.0 %collective-permute-done.6 = bf16[512,1024]{1,0:T(8,128)(2,1)S(1)} collective-permute-done((bf16[512,1024]{1,0:T(8,128)(2,1)S(1)}, bf16[512,1024]{1,0:T(8,128)(2,1)S(1)}, u32[]{:S(2)}, u32[]{:S(2)}) %collective-permute-start.6) | collective-permute-done | bytes 1048608 | tf_op jit(solution)/shard_map/ppermute | solution.py:248
  382.0 5.7 add_convert_fusion.1
  388.0 7.4 %convolution_convert_fusion.7 = bf16[512,1024]{1,0:T(8,128)(2,1)} fusion(bf16[2048,1024]{0,1:T(8,128)(2,1)} %all-gather.13.cloned.1.call-done, f32[512,2048]{1,0:T(8,128)} %copy-done.64, f32[2048]{0:T(1024)S(1)} %copy-done.38), kind=kOutput, calls=%fused_computation.58 | convolution fusion | flops 2158493696 | bytes 9445376 | tf_op jit(solution)/shard_map/dot_general | solution.py:285
  397.0 92.3 %all-gather.1 = f32[196608]{0:T(1024)} all-gather(f32[6144]{0:T(1024)S(1)} %add_dynamic-update-slice_fusion), channel_id=3, replica_groups=mesh['dp'=16,'tensor'=2] {'dp','tensor'}, dimensions={0}, use_global_device_ids=true | all-gather | bytes 811008 | tf_op jit(solution)/shard_map/all_gather | solution.py:296
  500.3 27.1 %attention_backward.1 = (bf16[1024,1536]{1,0:T(8,128)(2,1)S(1)}, f32[1,1536]{1,0:T(1,128)S(1)}) custom-call(f32[8]{0:T(128)S(1)} %multiply_exponential_fusion.slopes, bf16[1024,1536]{1,0:T(8,128)(2,1)S(1)} %pad_maximum_fusion.x, bf16[1024,512]{1,0:T(8,128)(2,1)S(1)} %pad_maximum_fusion.1.grad, s32[1024,1]{1,0:T(8,128)S(1)} %copy-done.3, s32[1,1024]{1,0:T(1,128)S(1)} %copy-done.4), custom_call_target="tpu_custom_call" | custom-call | flops 4026531840 | bytes 7340032 | tf_op jit(solution)/shard_map/attention_backward/pallas_call | solution.py:213
  535.1 5.0 convolution_convert_fusion.1
  541.1 5.4 add_add_fusion
  546.7 15.0 %collective-permute-done.7 = bf16[512,1024]{1,0:T(8,128)(2,1)} collective-permute-done((bf16[512,1024]{1,0:T(8,128)(2,1)}, bf16[512,1024]{1,0:T(8,128)(2,1)}, u32[]{:S(2)}, u32[]{:S(2)}) %collective-permute-start.7) | collective-permute-done | bytes 1048608 | tf_op jit(solution)/shard_map/ppermute | solution.py:248
  561.7 6.1 multiply_reduce_fusion.1
  567.9 66.9 %all-gather = f32[98304]{0:T(1024)S(1)} all-gather(f32[3072]{0:T(1024)S(1)} %pad_maximum_fusion.3), channel_id=2, replica_groups=mesh['dp'=16,'tensor'=2] {'dp','tensor'}, dimensions={0}, use_global_device_ids=true | all-gather | bytes 405504 | tf_op jit(solution)/shard_map/all_gather | solution.py:296
  (239 shorter events, 94.4 us)
Async XLA Ops:
  7.3 51.7 %all-gather.7.cloned.1.call-start = ((), (), s32[]{:S(2)}) async-start(), calls=%async_computation.4 | async-start | bytes 3342336 | tf_op jit(solution)/shard_map/all_gather | solution.py:399
  9.2 88.9 %all-gather.9.cloned.1.call-start = ((), (), s32[]{:S(2)}) async-start(), calls=%async_computation.5 | async-start | bytes 1114112 | tf_op jit(solution)/shard_map/all_gather | solution.py:400
  10.8 139.4 %all-gather.11.cloned.1.call-start = ((), (), s32[]{:S(2)}) async-start(), calls=%async_computation.6 | async-start | bytes 4456448 | tf_op jit(solution)/shard_map/all_gather | solution.py:401
  12.6 242.5 %reduce-scatter.11.cloned.1.call-start = ((), (), s32[]{:S(2)}) async-start(), calls=%async_computation.11 | async-start | bytes 4456448 | tf_op jit(solution)/shard_map/reduce_scatter | solution.py:497
  13.7 49.2 %collective-permute-start = (bf16[512,1024]{1,0:T(8,128)(2,1)S(1)}, bf16[512,1024]{1,0:T(8,128)(2,1)S(1)}, u32[]{:S(2)}, u32[]{:S(2)}) collective-permute-start(bf16[512,1024]{1,0:T(8,128)(2,1)S(1)} %add_convert_fusion.5), channel_id=1, source_target_pairs={{0,1},{1,0},{2,3},{3,2},{4,5},{5,4},{6,7},{7,6},{8,9},{9,8},{10,11... | collective-permute-start | bytes 3145736 | tf_op jit(solution)/shard_map/ppermute | solution.py:248
  101.3 26.3 %collective-permute-start.1 = (bf16[512,1024]{1,0:T(8,128)(2,1)}, bf16[512,1024]{1,0:T(8,128)(2,1)}, u32[]{:S(2)}, u32[]{:S(2)}) collective-permute-start(bf16[512,1024]{1,0:T(8,128)(2,1)} %convolution_convert_fusion.3), channel_id=1, source_target_pairs={{0,1},{1,0},{2,3},{3,2},{4,5},{5,4},{6,7},{7,6},{8,9},{9,8},{10,11... | collective-permute-start | bytes 3145736 | tf_op jit(solution)/shard_map/ppermute | solution.py:248
  104.0 71.5 %collective-permute-start.4 = (bf16[512,1024]{1,0:T(8,128)(2,1)}, bf16[512,1024]{1,0:T(8,128)(2,1)}, u32[]{:S(2)}, u32[]{:S(2)}) collective-permute-start(bf16[512,1024]{1,0:T(8,128)(2,1)} %get-tuple-element.113), channel_id=1, source_target_pairs={{0,1},{1,0},{2,3},{3,2},{4,5},{5,4},{6,7},{7,6},{8,9},{9,8},{10,11... | collective-permute-start | bytes 3145736 | tf_op jit(solution)/shard_map/ppermute | solution.py:248
  133.6 38.3 %collective-permute-start.2 = (bf16[512,1024]{1,0:T(8,128)(2,1)}, bf16[512,1024]{1,0:T(8,128)(2,1)}, u32[]{:S(2)}, u32[]{:S(2)}) collective-permute-start(bf16[512,1024]{1,0:T(8,128)(2,1)} %add_convert_fusion.4), channel_id=1, source_target_pairs={{0,1},{1,0},{2,3},{3,2},{4,5},{5,4},{6,7},{7,6},{8,9},{9,8},{10,11... | collective-permute-start | bytes 3145736 | tf_op jit(solution)/shard_map/ppermute | solution.py:248
  183.2 124.6 %all-gather.13.cloned.1.call-start = ((), (), s32[]{:S(2)}) async-start(), calls=%async_computation.7 | async-start | bytes 4456448 | tf_op jit(solution)/shard_map/all_gather | solution.py:402
  258.3 382.6 %reduce-scatter.7.cloned.1.call-start = ((), (), s32[]{:S(2)}) async-start(), calls=%async_computation.9 | async-start | bytes 1114112 | tf_op jit(solution)/shard_map/reduce_scatter | solution.py:495
  319.9 25.4 %collective-permute-start.5 = (bf16[512,1024]{1,0:T(8,128)(2,1)S(1)}, bf16[512,1024]{1,0:T(8,128)(2,1)S(1)}, u32[]{:S(2)}, u32[]{:S(2)}) collective-permute-start(bf16[512,1024]{1,0:T(8,128)(2,1)S(1)} %convolution_convert_fusion.5), channel_id=1, source_target_pairs={{0,1},{1,0},{2,3},{3,2},{4,5},{5,4},{6,7},{7,6},{8,9},{9,8},{10,11... | collective-permute-start | bytes 3145736 | tf_op jit(solution)/shard_map/ppermute | solution.py:248
  349.4 24.5 %collective-permute-start.6 = (bf16[512,1024]{1,0:T(8,128)(2,1)S(1)}, bf16[512,1024]{1,0:T(8,128)(2,1)S(1)}, u32[]{:S(2)}, u32[]{:S(2)}) collective-permute-start(bf16[512,1024]{1,0:T(8,128)(2,1)S(1)} %convert_element_type.149), channel_id=1, source_target_pairs={{0,1},{1,0},{2,3},{3,2},{4,5},{5,4},{6,7},{7,6},{8,9},{9,8},{10,11... | collective-permute-start | bytes 3145736 | tf_op jit(solution)/shard_map/ppermute | solution.py:248
  377.5 265.1 %reduce-scatter.9.cloned.1.call-start = ((), (), s32[]{:S(2)}) async-start(), calls=%async_computation.10 | async-start | bytes 4456448 | tf_op jit(solution)/shard_map/reduce_scatter | solution.py:496
  387.7 257.6 %reduce-scatter.5.cloned.1.call-start = ((), (), s32[]{:S(2)}) async-start(), calls=%async_computation.8 | async-start | bytes 3342336 | tf_op jit(solution)/shard_map/reduce_scatter | solution.py:494
  395.4 100.9 %copy-start.39 = (f32[1024]{0:T(1024)S(1)}, f32[1024]{0:T(1024)}, u32[]{:S(2)}) copy-start(f32[1024]{0:T(1024)} %param.65) | copy-start | bytes 12292
  395.4 100.9 %copy-start.40 = (f32[1024]{0:T(1024)S(1)}, f32[1024]{0:T(1024)}, u32[]{:S(2)}) copy-start(f32[1024]{0:T(1024)} %param.77) | copy-start | bytes 12292
  395.4 100.9 %copy-start.41 = (f32[1024]{0:T(1024)S(1)}, f32[1024]{0:T(1024)}, u32[]{:S(2)}) copy-start(f32[1024]{0:T(1024)} %param.76) | copy-start | bytes 12292
  395.4 100.9 %copy-start.42 = (f32[1024]{0:T(1024)S(1)}, f32[1024]{0:T(1024)}, u32[]{:S(2)}) copy-start(f32[1024]{0:T(1024)} %param.64) | copy-start | bytes 12292
  395.4 100.9 %copy-start.43 = (f32[1024]{0:T(1024)S(1)}, f32[1024]{0:T(1024)}, u32[]{:S(2)}) copy-start(f32[1024]{0:T(1024)} %param.73) | copy-start | bytes 12292
  395.4 100.9 %copy-start.44 = (f32[1024]{0:T(1024)S(1)}, f32[1024]{0:T(1024)}, u32[]{:S(2)}) copy-start(f32[1024]{0:T(1024)} %param.61) | copy-start | bytes 12292
  395.4 100.9 %copy-start.45 = (f32[1024]{0:T(1024)S(1)}, f32[1024]{0:T(1024)}, u32[]{:S(2)}) copy-start(f32[1024]{0:T(1024)} %param.69) | copy-start | bytes 12292
  395.4 100.9 %copy-start.46 = (f32[1024]{0:T(1024)S(1)}, f32[1024]{0:T(1024)}, u32[]{:S(2)}) copy-start(f32[1024]{0:T(1024)} %param.57) | copy-start | bytes 12292
  395.5 144.7 %collective-permute-start.3 = (bf16[512,1024]{1,0:T(8,128)(2,1)}, bf16[512,1024]{1,0:T(8,128)(2,1)}, u32[]{:S(2)}, u32[]{:S(2)}) collective-permute-start(bf16[512,1024]{1,0:T(8,128)(2,1)} %convolution_convert_fusion.7), channel_id=1, source_target_pairs={{0,1},{1,0},{2,3},{3,2},{4,5},{5,4},{6,7},{7,6},{8,9},{9,8},{10,11... | collective-permute-start | bytes 3145736 | tf_op jit(solution)/shard_map/ppermute | solution.py:248
  540.1 21.6 %collective-permute-start.7 = (bf16[512,1024]{1,0:T(8,128)(2,1)}, bf16[512,1024]{1,0:T(8,128)(2,1)}, u32[]{:S(2)}, u32[]{:S(2)}) collective-permute-start(bf16[512,1024]{1,0:T(8,128)(2,1)} %convolution_convert_fusion.1), channel_id=1, source_target_pairs={{0,1},{1,0},{2,3},{3,2},{4,5},{5,4},{6,7},{7,6},{8,9},{9,8},{10,11... | collective-permute-start | bytes 3145736 | tf_op jit(solution)/shard_map/ppermute | solution.py:248
  (60 other events, 1389.9 us)
Sparse Core Ops, SparseCore 0:
  10.9 48.0 all-gather.6
  61.7 36.2 all-gather.8
  100.8 49.3 all-gather.10
  183.3 71.7 reduce-scatter.10
  258.4 49.3 all-gather.12
  377.6 56.1 reduce-scatter.6
  437.7 72.5 reduce-scatter.8
  533.3 62.3 reduce-scatter.4
